TPU v7x, 32 devices: a whole 2x2x4 slice. The times are simulated.
32 devices in a mesh: tm: 16 (over z, y, x), sensor: 2 (over core).
Axes of the slice: x: 2, y: 2, z: 4, core: 2. Of those that a mesh axis runs over, the one named last changes fastest.
Arguments:
- sensor_rows: float32 [4096, 128], P('sensor'), may hold values from -0.12 to 0.12
- sensor_prec: float32 [4096], P('sensor'), may hold values from 0.5 to 2
- obs_sensor: int32 [8192], P(('tm', 'sensor')), may hold values from 0 to 2047
- obs_value: float32 [8192], P(('tm', 'sensor')), may hold values from -6 to 6
- obs_block: int32 [8192, 1], P(('tm', 'sensor')), may hold values from 0 to 15; in each aligned block of 256 rows (0 to 255, 256 to 511, ...) at most 32 rows name the same one
- obs_offset: int32 [8192], P(('tm', 'sensor')), may hold values from 0 to 63
- decay: float32 [1024, 128], P('tm'), may hold values from 0 to 1, as said below
- mix_raw: float32 [128, 128], replicated, may hold values from -1.2 to 1.2
- combine: float32 [128, 128], replicated, may hold values from -0.5 to 0.5
Outputs:
- smoothed: float32 [1024, 128], P('tm')
Inputs may be any that keep to these rules, and one draw needn't show every extreme that they name: `decay`: every factor lies in (0, 1]. `obs_block`: the rows of one device name one time block at most 32 times, and exactly 32 times for some block.
All inputs are finite; a program needn't handle non-finite values.
Results may differ from a plain program's by a relative error of at most 0.007.
Values may be sent and summed in bfloat16 or wider, within the bound.
A program may use at most 128 MiB of HBM per device.

v0:
```python
import functools
import math

import jax
import jax.numpy as jnp
from jax import lax
from jax.experimental import pallas as pl
from jax.experimental.pallas import tpu as pltpu
from jax.sharding import PartitionSpec as P

ROTATION_ITERS = 12
CHUNK = 8
F32, BF16 = jnp.float32, jnp.bfloat16
MESH = pl.DeviceIdType.MESH
NT = (((1,), (1,)), ((), ()))


def dot(x, y):
    return jnp.dot(x, y, preferred_element_type=F32)


def dot_nt(x, y):
    return lax.dot_general(x, y, NT, preferred_element_type=F32)


def cat(parts, axis):
    return jnp.concatenate(parts, axis=axis)


def split(x, n):
    parts = []
    for k in range(n):
        part = x.astype(BF16)
        parts.append(part)
        if k + 1 < n:
            x = x - part.astype(F32)
    return parts


def halves(z):
    w = z.shape[1] // 2
    return z[:, :w] + z[:, w:]


def lhs2(x):
    return cat(split(x, 2), 1)


def rhs2(y):
    row = cat(split(y, 2), 1)
    return cat([row, row], 0)


def rhs2_nt(y):
    a, b = split(y, 2)
    return cat([cat([a, a], 1), cat([b, b], 1)], 0)


def mm(x, y):
    return halves(dot(lhs2(x), rhs2(y)))


def mm_nt(x, y):
    return halves(dot_nt(lhs2(x), rhs2_nt(y)))


def polish(matrix):
    for _ in range(ROTATION_ITERS):
        a, b, c = split(matrix, 3)
        ab, ac = cat([a, b], 1), cat([a, c], 1)
        top = dot_nt(ab, cat([cat([a, a], 1), cat([b, b], 1)], 0))
        square = (dot_nt(ac, cat([c, a], 1)) + top[:, 128:]) + top[:, :128]
        p, q, r = split(square, 3)
        row = cat([a, b], 1)
        top = dot(cat([p, q], 1), cat([row, row], 0))
        cube = (dot(cat([p, r], 1), cat([c, a], 0)) + top[:, 128:]) + top[:, :128]
        matrix = 1.5 * matrix - 0.5 * cube
    return matrix


def kernel(
    inner, outer, cores,
    rows_ref, prec_ref, sens_ref, value_ref, block_ref, offset_ref, decay_ref, mix_ref, combine_ref,
    out_ref,
    part, got1, red1, got2, info, maps1, vecs1, maps2, vecs2, smooth,
    s_i1, r_i1, s_i2, r_i2, s_i3, r_i3, s_m1, r_m1, s_v1, r_v1, s_m2, r_m2, s_v2, r_v2,
):
    steps, width = decay_ref.shape
    half = steps // cores
    chunks = steps // CHUNK
    tm, core = lax.axis_index("tm"), lax.axis_index("sensor")
    mine, group = lax.rem(tm, inner), lax.div(tm, inner)
    spot = mine * cores + core
    spots = inner * cores

    def at_spot(s):
        return {"tm": group * inner + lax.div(s, cores), "sensor": lax.rem(s, cores)}

    def at_inner(k):
        return {"tm": group * inner + k, "sensor": core}

    def at_outer(k):
        return {"tm": k * inner + mine, "sensor": core}

    barrier = pltpu.get_barrier_semaphore()
    for r in range(1, spots):
        pl.semaphore_signal(barrier, inc=1, device_id=at_spot(lax.rem(spot + r, spots)), device_id_type=MESH)
    for r in range(1, outer):
        pl.semaphore_signal(barrier, inc=1, device_id=at_outer(lax.rem(group + r, outer)), device_id_type=MESH)

    obs = sens_ref.shape[1]
    column = jnp.broadcast_to(sens_ref[...].astype(F32), (width, obs)).T
    values = jnp.broadcast_to(value_ref[...], (width, obs)).T
    lane = lax.broadcasted_iota(jnp.int32, (obs, width), 1).astype(F32)
    hot, prec = [], jnp.zeros((obs, width), F32)
    for k in range(rows_ref.shape[0] // width):
        hit = (column - float(k * width)) == lane
        hot.append(jnp.where(hit, 1.0, 0.0).astype(BF16))
        prec = prec + jnp.where(hit, prec_ref[:, k * width : (k + 1) * width], 0.0)
    gain = values * jnp.sum(prec, axis=1, keepdims=True)
    picked = halves(dot(cat(hot, 1), lhs2(rows_ref[...])))
    contrib = (picked * gain).astype(BF16)

    block, offset = block_ref[...], offset_ref[...]
    place = ((lax.rem(block, inner) * cores + lax.div(offset, half)) * outer + lax.div(block, inner)) * half
    place = place + lax.rem(offset, half)
    size = outer * half
    for s in range(spots):
        line = lax.broadcasted_iota(jnp.int32, (size, obs), 0) + s * size
        part[s] = dot(jnp.where(line == place, 1.0, 0.0).astype(BF16), contrib).astype(BF16)

    pl.semaphore_wait(barrier, spots - 1 + outer - 1)

    sent1 = []
    for r in range(1, spots):
        to = lax.rem(spot + r, spots)
        copy = pltpu.make_async_remote_copy(
            part.at[to], got1.at[spot], s_i1.at[r], r_i1.at[r], device_id=at_spot(to), device_id_type=MESH
        )
        copy.start()
        sent1.append(copy)
    got1[spot] = part[spot]

    rotation = polish(mix_ref[...])
    turned = rotation.T
    ahead, back = rhs2(turned), rhs2(rotation)

    for copy in sent1:
        copy.wait()
    total = got1[0].astype(F32)
    for s in range(1, spots):
        total = total + got1[s].astype(F32)
    red1[...] = total.reshape(outer, half, width)
    sent2 = []
    for r in range(1, outer):
        to = lax.rem(group + r, outer)
        copy = pltpu.make_async_remote_copy(
            red1.at[to], got2.at[group], s_i2.at[r], r_i2.at[r], device_id=at_outer(to), device_id_type=MESH
        )
        copy.start()
        sent2.append(copy)
    got2[group] = red1[group]

    def decay_row(t):
        return decay_ref[t : t + 1, :]

    maps = [turned * decay_row(c * CHUNK) for c in range(chunks)]
    for j in range(1, CHUNK):
        maps = [halves(dot(lhs2(m), ahead)) * decay_row(c * CHUNK + j) for c, m in enumerate(maps)]

    for copy in sent2:
        copy.wait()
    total = got2[0]
    for k in range(1, outer):
        total = total + got2[k]
    info[core] = total
    other = cores - 1 - core
    copy3 = pltpu.make_async_remote_copy(
        info.at[core], info.at[core], s_i3, r_i3, device_id={"tm": tm, "sensor": other}, device_id_type=MESH
    )
    copy3.start()

    levels = [maps]
    while len(levels[-1]) > 1:
        last = levels[-1]
        levels.append([mm(last[k], last[k + 1]) for k in range(0, len(last), 2)])

    def exchange(source, slots, me, count, send, recv, place_of):
        copies = []
        for r in range(1, count):
            copy = pltpu.make_async_remote_copy(
                source, slots.at[me], send.at[r], recv.at[r],
                device_id=place_of(lax.rem(me + r, count)), device_id_type=MESH,
            )
            copy.start()
            copies.append(copy)
        return copies

    maps1[mine] = levels[-1][0]
    sent_m1 = exchange(maps1.at[mine], maps1, mine, inner, s_m1, r_m1, at_inner)

    copy3.wait()

    def strided(ref, j):
        return ref[pl.ds(j, chunks, stride=CHUNK), :]

    for c in range(cores):
        smooth[c * half : (c + 1) * half, :] = info[c]
    news = [strided(smooth, j) for j in range(CHUNK)]
    fades = [strided(decay_ref, j) for j in range(CHUNK)]

    def forward_scan(enter):
        out, state = [], enter
        for j in range(CHUNK):
            if state is None:
                state = news[j]
            else:
                state = halves(dot(lhs2(state), ahead)) * fades[j] + news[j]
            out.append(state)
        return out

    def backward_scan(arrive):
        out, message = [None] * CHUNK, arrive
        for j in reversed(range(CHUNK)):
            value = news[j] if message is None else news[j] + message
            out[j] = value
            message = halves(dot(lhs2(value * fades[j]), back))
        return out, message

    first = forward_scan(None)[-1]
    second = backward_scan(None)[1]
    fronts = [[first[c : c + 1] for c in range(chunks)]]
    tails = [[second[c : c + 1] for c in range(chunks)]]
    for depth in range(len(levels) - 1):
        f, b, m = fronts[-1], tails[-1], levels[depth]
        fronts.append([mm(f[k], m[k + 1]) + f[k + 1] for k in range(0, len(m), 2)])
        tails.append([mm_nt(b[k + 1], m[k]) + b[k] for k in range(0, len(m), 2)])

    vecs1[mine] = cat([fronts[-1][0], tails[-1][0], jnp.zeros((6, width), F32)], 0)
    sent_v1 = exchange(vecs1.at[mine], vecs1, mine, inner, s_v1, r_v1, at_inner)
    for copy in sent_m1:
        copy.wait()
    near = [maps1[k] for k in range(inner)]
    tree = [near]
    while len(tree[-1]) > 1:
        last = tree[-1]
        tree.append([mm(last[k], last[k + 1]) for k in range(0, len(last), 2)])
    maps2[group] = tree[-1][0]
    sent_m2 = exchange(maps2.at[group], maps2, group, outer, s_m2, r_m2, at_outer)
    for copy in sent_v1:
        copy.wait()
    f = [vecs1[k][0:1] for k in range(inner)]
    b = [vecs1[k][1:2] for k in range(inner)]
    near_f, near_b = f, b
    for depth in range(len(tree) - 1):
        m = tree[depth]
        f, b = (
            [mm(f[k], m[k + 1]) + f[k + 1] for k in range(0, len(m), 2)],
            [mm_nt(b[k + 1], m[k]) + b[k] for k in range(0, len(m), 2)],
        )
    vecs2[group] = cat([f[0], b[0], jnp.zeros((6, width), F32)], 0)
    sent_v2 = exchange(vecs2.at[group], vecs2, group, outer, s_v2, r_v2, at_outer)
    for copy in sent_m2 + sent_v2:
        copy.wait()

    enter = jnp.zeros((1, width), F32)
    arrive = jnp.zeros((1, width), F32)
    for k in range(outer - 1):
        enter = jnp.where(k < group, mm(enter, maps2[k]) + vecs2[k][0:1], enter)
        j = outer - 1 - k
        arrive = jnp.where(j > group, mm_nt(arrive, maps2[j]) + vecs2[j][1:2], arrive)
    for k in range(inner - 1):
        enter = jnp.where(k < mine, mm(enter, near[k]) + near_f[k], enter)
        j = inner - 1 - k
        arrive = jnp.where(j > mine, mm_nt(arrive, near[j]) + near_b[j], arrive)

    starts, ends = [enter], [arrive]
    for depth in reversed(range(len(levels) - 1)):
        m, f, b = levels[depth], fronts[depth], tails[depth]
        starts = [x for k, e in enumerate(starts) for x in (e, mm(e, m[2 * k]) + f[2 * k])]
        ends = [x for k, e in enumerate(ends) for x in (mm_nt(e, m[2 * k + 1]) + b[2 * k + 1], e)]
    start, end = cat(starts, 0), cat(ends, 0)
    forward = forward_scan(start)
    backward = backward_scan(end)[0]
    for j in range(CHUNK):
        smooth[pl.ds(j, chunks, stride=CHUNK), :] = forward[j] + backward[j] - news[j]
    out_ref[...] = mm(smooth[...], combine_ref[...])


def local(sensor_rows, sensor_prec, obs_sensor, obs_value, obs_block, obs_offset, decay, mix_raw, combine):
    peers, cores = lax.axis_size("tm"), lax.axis_size("sensor")
    inner = 1 << (int(math.log2(peers)) // 2)
    outer = peers // inner
    steps, width = decay.shape
    half = steps // cores
    spots = inner * cores
    dma = pltpu.SemaphoreType.DMA
    obs = obs_sensor.shape[0]
    return pl.pallas_call(
        functools.partial(kernel, inner, outer, cores),
        out_shape=jax.ShapeDtypeStruct((steps, width), F32),
        in_specs=[pl.BlockSpec(memory_space=pltpu.VMEM)] * 9,
        out_specs=pl.BlockSpec(memory_space=pltpu.VMEM),
        scratch_shapes=[
            pltpu.VMEM((spots, outer * half, width), BF16),
            pltpu.VMEM((spots, outer * half, width), BF16),
            pltpu.VMEM((outer, half, width), F32),
            pltpu.VMEM((outer, half, width), F32),
            pltpu.VMEM((cores, half, width), F32),
            pltpu.VMEM((inner, width, width), F32),
            pltpu.VMEM((inner, 8, width), F32),
            pltpu.VMEM((outer, width, width), F32),
            pltpu.VMEM((outer, 8, width), F32),
            pltpu.VMEM((steps, width), F32),
            dma((spots,)), dma((spots,)), dma((outer,)), dma((outer,)), dma, dma,
            dma((inner,)), dma((inner,)), dma((inner,)), dma((inner,)),
            dma((outer,)), dma((outer,)), dma((outer,)), dma((outer,)),
        ],
        compiler_params=pltpu.CompilerParams(
            collective_id=0, has_side_effects=True, vmem_limit_bytes=48 * 1024 * 1024
        ),
    )(
        sensor_rows, sensor_prec.reshape(1, -1), obs_sensor.reshape(1, obs), obs_value.reshape(1, obs),
        obs_block.reshape(1, obs), obs_offset.reshape(1, obs), decay, mix_raw, combine,
    )


def solution(mesh):
    placed = (
        P("sensor", None), P("sensor"), P(("tm", "sensor")), P(("tm", "sensor")),
        P(("tm", "sensor"), None), P(("tm", "sensor")), P("tm", None), P(), P(),
    )
    return jax.shard_map(local, mesh=mesh, in_specs=placed, out_specs=P("tm", None), check_vma=False)
```

profile of v0, /device:TPU:0, one launch (start us, length us, event | category | flops | bytes accessed | tf_op | source)
XLA Modules:
  0.0 35.9 jit_solution(9837354797334758328)
XLA Ops:
  0.0 0.0 copy-start.4
  0.0 0.0 copy-start.5
  0.0 0.7 %copy-done.4 = f32[2048]{0:T(1024)S(1)} copy-done((f32[2048]{0:T(1024)S(1)}, f32[2048]{0:T(1024)}, u32[]{:S(2)}) %copy-start.4) | copy-done | bytes 8216
  0.7 0.0 copy-done.5
  0.7 0.0 copy-start
  0.7 1.2 %copy-done = f32[2048,128]{1,0:T(8,128)S(1)} copy-done((f32[2048,128]{1,0:T(8,128)S(1)}, f32[2048,128]{1,0:T(8,128)}, u32[]{:S(2)}) %copy-start) | copy-done | bytes 1048600
  1.9 0.0 copy-start.1
  1.9 0.8 %copy-done.1 = f32[128,128]{1,0:T(8,128)S(1)} copy-done((f32[128,128]{1,0:T(8,128)S(1)}, f32[128,128]{1,0:T(8,128)}, u32[]{:S(2)}) %copy-start.1) | copy-done | bytes 65560
  2.8 0.0 copy-start.2
  2.8 0.8 %copy-done.2 = f32[128,128]{1,0:T(8,128)S(1)} copy-done((f32[128,128]{1,0:T(8,128)S(1)}, f32[128,128]{1,0:T(8,128)}, u32[]{:S(2)}) %copy-start.2) | copy-done | bytes 65560
  3.6 0.0 copy-start.3
  3.6 0.8 %copy-done.3 = f32[64,128]{1,0:T(8,128)S(1)} copy-done((f32[64,128]{1,0:T(8,128)S(1)}, f32[64,128]{1,0:T(8,128)}, u32[]{:S(2)}) %copy-start.3) | copy-done | bytes 32792
  4.4 0.0 copy-start.6
  4.4 0.7 %copy-done.6 = f32[256]{0:T(256)S(1)} copy-done((f32[256]{0:T(256)S(1)}, f32[256]{0:T(256)}, u32[]{:S(2)}) %copy-start.6) | copy-done | bytes 1048
  5.0 0.0 copy-start.7
  5.0 0.7 %copy-done.7 = s32[256,1]{0,1:T(1,128)S(1)} copy-done((s32[256,1]{0,1:T(1,128)S(1)}, s32[256,1]{0,1:T(1,128)}, u32[]{:S(2)}) %copy-start.7) | copy-done | bytes 1048
  5.7 0.0 copy-start.8
  5.7 0.7 %copy-done.8 = s32[256]{0:T(256)S(1)} copy-done((s32[256]{0:T(256)S(1)}, s32[256]{0:T(256)}, u32[]{:S(2)}) %copy-start.8) | copy-done | bytes 1048
  6.4 28.9 %shard_map.91 = f32[64,128]{1,0:T(8,128)S(1)} custom-call(f32[2048,128]{1,0:T(8,128)S(1)} %copy-done, f32[1,2048]{1,0:T(1,128)S(1)} %bitcast.5, s32[1,256]{1,0:T(1,128)S(1)} %bitcast.6, f32[1,256]{1,0:T(1,128)S(1)} %bitcast.7, s32[1,256]{1,0:T(1,128)S(1)} %bitcast.8, s32[1,256]{1,0:T(1,128)S(1)} %bitcast.9, f32[64,128]{1,0:T(8,128)S(1)} %copy-done.3, ...), custom_call_target="tpu_custom_call" | custom-call | tf_op jit(solution)/shard_map/pallas_call | solution.py:299
  35.3 0.6 %copy.11 = f32[64,128]{1,0:T(8,128)} copy(f32[64,128]{1,0:T(8,128)S(1)} %shard_map.91) | data formatting | bytes 65536
Async XLA Ops:
  0.0 0.7 %copy-start.4 = (f32[2048]{0:T(1024)S(1)}, f32[2048]{0:T(1024)}, u32[]{:S(2)}) copy-start(f32[2048]{0:T(1024)} %param.10) | copy-start | bytes 24580
  0.0 0.7 %copy-start.5 = (s32[256]{0:T(256)S(1)}, s32[256]{0:T(256)}, u32[]{:S(2)}) copy-start(s32[256]{0:T(256)} %param.11) | copy-start | bytes 3076
  0.7 1.2 %copy-start = (f32[2048,128]{1,0:T(8,128)S(1)}, f32[2048,128]{1,0:T(8,128)}, u32[]{:S(2)}) copy-start(f32[2048,128]{1,0:T(8,128)} %rows_ref.1) | copy-start | bytes 3145732
  1.9 0.8 %copy-start.1 = (f32[128,128]{1,0:T(8,128)S(1)}, f32[128,128]{1,0:T(8,128)}, u32[]{:S(2)}) copy-start(f32[128,128]{1,0:T(8,128)} %mix_ref.1) | copy-start | bytes 196612
  2.8 0.8 %copy-start.2 = (f32[128,128]{1,0:T(8,128)S(1)}, f32[128,128]{1,0:T(8,128)}, u32[]{:S(2)}) copy-start(f32[128,128]{1,0:T(8,128)} %combine_ref.1) | copy-start | bytes 196612
  3.6 0.8 %copy-start.3 = (f32[64,128]{1,0:T(8,128)S(1)}, f32[64,128]{1,0:T(8,128)}, u32[]{:S(2)}) copy-start(f32[64,128]{1,0:T(8,128)} %decay_ref.1) | copy-start | bytes 98308
  4.4 0.7 %copy-start.6 = (f32[256]{0:T(256)S(1)}, f32[256]{0:T(256)}, u32[]{:S(2)}) copy-start(f32[256]{0:T(256)} %param.12) | copy-start | bytes 3076
  5.0 0.7 %copy-start.7 = (s32[256,1]{0,1:T(1,128)S(1)}, s32[256,1]{0,1:T(1,128)}, u32[]{:S(2)}) copy-start(s32[256,1]{0,1:T(1,128)} %param.13) | copy-start | bytes 3076
  5.7 0.7 %copy-start.8 = (s32[256]{0:T(256)S(1)}, s32[256]{0:T(256)}, u32[]{:S(2)}) copy-start(s32[256]{0:T(256)} %param.14) | copy-start | bytes 3076
where the time goes:
time: 36.3 us; the launch traced here: 35.9 us
  Pallas kernels  28.9 us (80%)
  local copies, waits for them, and re-layouts  7.01 us (19%)
    pallas_call x1, Pallas kernels, local(): pl.pallas_call(functools.partial(kernel, inner, outer, cores), out_shape=...  28.9 us
    unnamed x19, local copies, waits for them, and re-layouts  7.01 us

commit v1 on v0

--- a/solution.py
+++ b/solution.py
@@ -64,27 +64,33 @@
     return halves(dot_nt(lhs2(x), rhs2_nt(y)))
 
 
-def polish(matrix):
-    for _ in range(ROTATION_ITERS):
-        a, b, c = split(matrix, 3)
-        ab, ac = cat([a, b], 1), cat([a, c], 1)
-        top = dot_nt(ab, cat([cat([a, a], 1), cat([b, b], 1)], 0))
-        square = (dot_nt(ac, cat([c, a], 1)) + top[:, 128:]) + top[:, :128]
-        p, q, r = split(square, 3)
-        row = cat([a, b], 1)
-        top = dot(cat([p, q], 1), cat([row, row], 0))
-        cube = (dot(cat([p, r], 1), cat([c, a], 0)) + top[:, 128:]) + top[:, :128]
-        matrix = 1.5 * matrix - 0.5 * cube
-    return matrix
+def polish_step(matrix):
+    a, b, c = split(matrix, 3)
+    ab, ac = cat([a, b], 1), cat([a, c], 1)
+    top = dot_nt(ab, cat([cat([a, a], 1), cat([b, b], 1)], 0))
+    square = (dot_nt(ac, cat([c, a], 1)) + top[:, 128:]) + top[:, :128]
+    p, q, r = split(square, 3)
+    top = dot(cat([p, q], 1), cat([ab, ab], 0))
+    cube = (dot(cat([p, r], 1), cat([c, a], 0)) + top[:, 128:]) + top[:, :128]
+    return 1.5 * matrix - 0.5 * cube
 
 
 def kernel(
-    inner, outer, cores,
-    rows_ref, prec_ref, sens_ref, value_ref, block_ref, offset_ref, decay_ref, mix_ref, combine_ref,
+    inner, outer, cores, early,
+    rows_hbm, prec_hbm, sens_hbm, value_hbm, block_hbm, offset_hbm, decay_hbm, mix_hbm, combine_hbm,
     out_ref,
-    part, got1, red1, got2, info, maps1, vecs1, maps2, vecs2, smooth,
+    rows_ref, prec_ref, sens_ref, value_ref, block_ref, offset_ref, decay_ref, mix_ref, combine_ref, loads,
+    part, got1, red1, got2, info, maps1, vecs1, maps2, vecs2, smooth, pairs, rows2,
     s_i1, r_i1, s_i2, r_i2, s_i3, r_i3, s_m1, r_m1, s_v1, r_v1, s_m2, r_m2, s_v2, r_v2,
 ):
+    sources = (mix_hbm, sens_hbm, value_hbm, prec_hbm, block_hbm, offset_hbm, rows_hbm, decay_hbm, combine_hbm)
+    targets = (mix_ref, sens_ref, value_ref, prec_ref, block_ref, offset_ref, rows_ref, decay_ref, combine_ref)
+    copies_in = []
+    for k, (source, target) in enumerate(zip(sources, targets)):
+        copy = pltpu.make_async_copy(source, target, loads.at[k])
+        copy.start()
+        copies_in.append(copy)
+
     steps, width = decay_ref.shape
     half = steps // cores
     chunks = steps // CHUNK
@@ -108,26 +114,39 @@
     for r in range(1, outer):
         pl.semaphore_signal(barrier, inc=1, device_id=at_outer(lax.rem(group + r, outer)), device_id_type=MESH)
 
+    for copy in copies_in:
+        copy.wait()
+
+    matrix = mix_ref[...]
+    left = ROTATION_ITERS
+
     obs = sens_ref.shape[1]
     column = jnp.broadcast_to(sens_ref[...].astype(F32), (width, obs)).T
     values = jnp.broadcast_to(value_ref[...], (width, obs)).T
     lane = lax.broadcasted_iota(jnp.int32, (obs, width), 1).astype(F32)
-    hot, prec = [], jnp.zeros((obs, width), F32)
-    for k in range(rows_ref.shape[0] // width):
-        hit = (column - float(k * width)) == lane
-        hot.append(jnp.where(hit, 1.0, 0.0).astype(BF16))
-        prec = prec + jnp.where(hit, prec_ref[:, k * width : (k + 1) * width], 0.0)
+    tiles = rows_ref.shape[0] // width
+    picked, prec = jnp.zeros((obs, 2 * width), F32), jnp.zeros((obs, width), F32)
+    for k in range(0, tiles, 2):
+        hot = []
+        for t in (k, k + 1):
+            hit = (column - float(t * width)) == lane
+            hot.append(jnp.where(hit, 1.0, 0.0).astype(BF16))
+            prec = prec + jnp.where(hit, prec_ref[:, t * width : (t + 1) * width], 0.0)
+        picked = picked + dot(cat(hot, 1), lhs2(rows_ref[k * width : (k + 2) * width, :]))
+        if k % 4 == 0 and ROTATION_ITERS - left < early - 2:
+            matrix, left = polish_step(matrix), left - 1
     gain = values * jnp.sum(prec, axis=1, keepdims=True)
-    picked = halves(dot(cat(hot, 1), lhs2(rows_ref[...])))
-    contrib = (picked * gain).astype(BF16)
+    contrib = (halves(picked) * gain).astype(BF16)
 
     block, offset = block_ref[...], offset_ref[...]
     place = ((lax.rem(block, inner) * cores + lax.div(offset, half)) * outer + lax.div(block, inner)) * half
     place = place + lax.rem(offset, half)
     size = outer * half
+    line = lax.broadcasted_iota(jnp.int32, (size, obs), 0)
     for s in range(spots):
-        line = lax.broadcasted_iota(jnp.int32, (size, obs), 0) + s * size
-        part[s] = dot(jnp.where(line == place, 1.0, 0.0).astype(BF16), contrib).astype(BF16)
+        part[s] = dot(jnp.where(line == place - s * size, 1.0, 0.0).astype(BF16), contrib).astype(BF16)
+        if s % (spots // 2) == 0 and ROTATION_ITERS - left < early:
+            matrix, left = polish_step(matrix), left - 1
 
     pl.semaphore_wait(barrier, spots - 1 + outer - 1)
 
@@ -141,9 +160,21 @@
         sent1.append(copy)
     got1[spot] = part[spot]
 
-    rotation = polish(mix_ref[...])
+    for _ in range(left):
+        matrix = polish_step(matrix)
+    rotation = matrix
     turned = rotation.T
     ahead, back = rhs2(turned), rhs2(rotation)
+
+    def decay_row(t):
+        return decay_ref[t : t + 1, :]
+
+    def advance(maps, j):
+        return [halves(dot(lhs2(m), ahead)) * decay_row(c * CHUNK + j) for c, m in enumerate(maps)]
+
+    maps = [turned * decay_row(c * CHUNK) for c in range(chunks)]
+    for j in range(1, 3):
+        maps = advance(maps, j)
 
     for copy in sent1:
         copy.wait()
@@ -161,13 +192,8 @@
         sent2.append(copy)
     got2[group] = red1[group]
 
-    def decay_row(t):
-        return decay_ref[t : t + 1, :]
-
-    maps = [turned * decay_row(c * CHUNK) for c in range(chunks)]
-    for j in range(1, CHUNK):
-        maps = [halves(dot(lhs2(m), ahead)) * decay_row(c * CHUNK + j) for c, m in enumerate(maps)]
-
+    for j in range(3, CHUNK):
+        maps = advance(maps, j)
     for copy in sent2:
         copy.wait()
     total = got2[0]
@@ -196,7 +222,7 @@
             copies.append(copy)
         return copies
 
-    maps1[mine] = levels[-1][0]
+    maps1[mine] = levels[-1][0].astype(maps1.dtype)
     sent_m1 = exchange(maps1.at[mine], maps1, mine, inner, s_m1, r_m1, at_inner)
 
     copy3.wait()
@@ -224,7 +250,8 @@
         for j in reversed(range(CHUNK)):
             value = news[j] if message is None else news[j] + message
             out[j] = value
-            message = halves(dot(lhs2(value * fades[j]), back))
+            if j > 0 or arrive is None:
+                message = halves(dot(lhs2(value * fades[j]), back))
         return out, message
 
     first = forward_scan(None)[-1]
@@ -236,43 +263,75 @@
         fronts.append([mm(f[k], m[k + 1]) + f[k + 1] for k in range(0, len(m), 2)])
         tails.append([mm_nt(b[k + 1], m[k]) + b[k] for k in range(0, len(m), 2)])
 
-    vecs1[mine] = cat([fronts[-1][0], tails[-1][0], jnp.zeros((6, width), F32)], 0)
+    def eight(f, b):
+        return cat([f, b, jnp.zeros((6, width), F32)], 0)
+
+    vecs1[mine] = eight(fronts[-1][0], tails[-1][0])
     sent_v1 = exchange(vecs1.at[mine], vecs1, mine, inner, s_v1, r_v1, at_inner)
     for copy in sent_m1:
         copy.wait()
-    near = [maps1[k] for k in range(inner)]
-    tree = [near]
-    while len(tree[-1]) > 1:
+
+    tree = [[maps1[k].astype(F32) for k in range(inner)]]
+    bases, base = [], 0
+    while len(tree[-1]) > (1 if outer > 2 else 2):
         last = tree[-1]
         tree.append([mm(last[k], last[k + 1]) for k in range(0, len(last), 2)])
-    maps2[group] = tree[-1][0]
-    sent_m2 = exchange(maps2.at[group], maps2, group, outer, s_m2, r_m2, at_outer)
+        bases.append(base)
+        for k, m in enumerate(tree[-1]):
+            pairs[base + k] = m
+        base += len(tree[-1])
+    sent_m2 = []
+    if outer > 2:
+        maps2[group] = tree[-1][0]
+        sent_m2 = exchange(maps2.at[group], maps2, group, outer, s_m2, r_m2, at_outer)
     for copy in sent_v1:
         copy.wait()
     f = [vecs1[k][0:1] for k in range(inner)]
     b = [vecs1[k][1:2] for k in range(inner)]
-    near_f, near_b = f, b
-    for depth in range(len(tree) - 1):
+    depths, base = inner.bit_length() - 1, 0
+    rows2_bases = []
+    for depth in range(depths):
         m = tree[depth]
         f, b = (
             [mm(f[k], m[k + 1]) + f[k + 1] for k in range(0, len(m), 2)],
             [mm_nt(b[k + 1], m[k]) + b[k] for k in range(0, len(m), 2)],
         )
-    vecs2[group] = cat([f[0], b[0], jnp.zeros((6, width), F32)], 0)
+        rows2_bases.append(base)
+        for k in range(len(f)):
+            rows2[base + k] = eight(f[k], b[k])
+        base += len(f)
+    vecs2[group] = eight(f[0], b[0])
     sent_v2 = exchange(vecs2.at[group], vecs2, group, outer, s_v2, r_v2, at_outer)
+
+    eye = (
+        lax.broadcasted_iota(jnp.int32, (width + 8, width), 0) == lax.broadcasted_iota(jnp.int32, (width + 8, width), 1)
+    ).astype(F32)
+    to_here, from_here = eye, eye
+    for depth in reversed(range(depths)):
+        node = lax.div(mine, 1 << depth)
+        bit = lax.rem(node, 2)
+        even = node - bit
+        if depth == 0:
+            m0, m1, v0, v1 = maps1[even].astype(F32), maps1[even + 1].astype(F32), vecs1[even], vecs1[even + 1]
+        else:
+            m0, m1 = pairs[bases[depth - 1] + even], pairs[bases[depth - 1] + even + 1]
+            v0, v1 = rows2[rows2_bases[depth - 1] + even], rows2[rows2_bases[depth - 1] + even + 1]
+        pad = jnp.zeros((width, width), F32)
+        to_here = jnp.where(bit == 1, mm(to_here, m0) + cat([pad, v0], 0), to_here)
+        from_here = jnp.where(bit == 0, mm_nt(from_here, m1) + cat([pad, v1], 0), from_here)
+
     for copy in sent_m2 + sent_v2:
         copy.wait()
 
-    enter = jnp.zeros((1, width), F32)
-    arrive = jnp.zeros((1, width), F32)
-    for k in range(outer - 1):
+    zero = jnp.zeros((1, width), F32)
+    enter = jnp.where(group > 0, vecs2[0][0:1], zero)
+    arrive = jnp.where(group < outer - 1, vecs2[outer - 1][1:2], zero)
+    for k in range(1, outer - 1):
         enter = jnp.where(k < group, mm(enter, maps2[k]) + vecs2[k][0:1], enter)
         j = outer - 1 - k
         arrive = jnp.where(j > group, mm_nt(arrive, maps2[j]) + vecs2[j][1:2], arrive)
-    for k in range(inner - 1):
-        enter = jnp.where(k < mine, mm(enter, near[k]) + near_f[k], enter)
-        j = inner - 1 - k
-        arrive = jnp.where(j > mine, mm_nt(arrive, near[j]) + near_b[j], arrive)
+    enter = mm(enter, to_here[:width]) + to_here[width : width + 1]
+    arrive = mm(arrive, from_here[:width]) + from_here[width + 1 : width + 2]
 
     starts, ends = [enter], [arrive]
     for depth in reversed(range(len(levels) - 1)):
@@ -280,49 +339,61 @@
         starts = [x for k, e in enumerate(starts) for x in (e, mm(e, m[2 * k]) + f[2 * k])]
         ends = [x for k, e in enumerate(ends) for x in (mm_nt(e, m[2 * k + 1]) + b[2 * k + 1], e)]
     start, end = cat(starts, 0), cat(ends, 0)
-    forward = forward_scan(start)
+    forward = forward_scan_from(start, ahead, fades, news)
     backward = backward_scan(end)[0]
     for j in range(CHUNK):
         smooth[pl.ds(j, chunks, stride=CHUNK), :] = forward[j] + backward[j] - news[j]
     out_ref[...] = mm(smooth[...], combine_ref[...])
 
 
+def forward_scan_from(state, ahead, fades, news):
+    out = []
+    for fade, new in zip(fades, news):
+        state = halves(dot(lhs2(state), ahead)) * fade + new
+        out.append(state)
+    return out
+
+
 def local(sensor_rows, sensor_prec, obs_sensor, obs_value, obs_block, obs_offset, decay, mix_raw, combine):
     peers, cores = lax.axis_size("tm"), lax.axis_size("sensor")
-    inner = 1 << (int(math.log2(peers)) // 2)
+    inner = min(8, peers // 2)
     outer = peers // inner
     steps, width = decay.shape
     half = steps // cores
     spots = inner * cores
     dma = pltpu.SemaphoreType.DMA
     obs = obs_sensor.shape[0]
+    arrays = (
+        sensor_rows, sensor_prec.reshape(1, -1), obs_sensor.reshape(1, obs), obs_value.reshape(1, obs),
+        obs_block.reshape(1, obs), obs_offset.reshape(1, obs), decay, mix_raw, combine,
+    )
     return pl.pallas_call(
-        functools.partial(kernel, inner, outer, cores),
+        functools.partial(kernel, inner, outer, cores, 6),
         out_shape=jax.ShapeDtypeStruct((steps, width), F32),
-        in_specs=[pl.BlockSpec(memory_space=pltpu.VMEM)] * 9,
+        in_specs=[pl.BlockSpec(memory_space=pltpu.HBM)] * 9,
         out_specs=pl.BlockSpec(memory_space=pltpu.VMEM),
-        scratch_shapes=[
+        scratch_shapes=[pltpu.VMEM(x.shape, x.dtype) for x in arrays] + [
+            dma((9,)),
             pltpu.VMEM((spots, outer * half, width), BF16),
             pltpu.VMEM((spots, outer * half, width), BF16),
             pltpu.VMEM((outer, half, width), F32),
             pltpu.VMEM((outer, half, width), F32),
             pltpu.VMEM((cores, half, width), F32),
-            pltpu.VMEM((inner, width, width), F32),
+            pltpu.VMEM((inner, width, width), BF16),
             pltpu.VMEM((inner, 8, width), F32),
             pltpu.VMEM((outer, width, width), F32),
             pltpu.VMEM((outer, 8, width), F32),
             pltpu.VMEM((steps, width), F32),
+            pltpu.VMEM((inner, width, width), F32),
+            pltpu.VMEM((inner, 8, width), F32),
             dma((spots,)), dma((spots,)), dma((outer,)), dma((outer,)), dma, dma,
             dma((inner,)), dma((inner,)), dma((inner,)), dma((inner,)),
             dma((outer,)), dma((outer,)), dma((outer,)), dma((outer,)),
         ],
         compiler_params=pltpu.CompilerParams(
-            collective_id=0, has_side_effects=True, vmem_limit_bytes=48 * 1024 * 1024
+            collective_id=0, has_side_effects=True, vmem_limit_bytes=60 * 1024 * 1024
         ),
-    )(
-        sensor_rows, sensor_prec.reshape(1, -1), obs_sensor.reshape(1, obs), obs_value.reshape(1, obs),
-        obs_block.reshape(1, obs), obs_offset.reshape(1, obs), decay, mix_raw, combine,
-    )
+    )(*arrays)
 
 
 def solution(mesh):

time: 36.3 us -> 31 us (0.85)
  local copies, waits for them, and re-layouts: 7.01 us -> 1.38 us
  Pallas kernels: 28.9 us -> 29.4 us
    unnamed x19 -> x1, local copies, waits for them, and re-layouts: 7.01 us -> 1.38 us
    pallas_call x1, Pallas kernels: 28.9 us -> 29.4 us  [local(): pl.pallas_call(functools.partial(kernel, inner, outer, cores, 6), out_sha...]
where the time goes in v1:
time: 31 us; the launch traced here: 30.8 us
  Pallas kernels  29.4 us (95%)
  local copies, waits for them, and re-layouts  1.38 us (4%)
    pallas_call x1, Pallas kernels, local(): pl.pallas_call(functools.partial(kernel, inner, outer, cores, 6), out_sha...  29.4 us
    unnamed x1, local copies, waits for them, and re-layouts  1.38 us

profile of v1, /device:TPU:0, one launch (start us, length us, event | category | flops | bytes accessed | tf_op | source)
XLA Modules:
  0.0 30.8 jit_solution(372244370291162467)
XLA Ops:
  0.0 29.4 %shard_map.91 = f32[64,128]{1,0:T(8,128)} custom-call(f32[2048,128]{1,0:T(8,128)} %rows_hbm.1, f32[1,2048]{1,0:T(1,128)} %bitcast.5, s32[1,256]{1,0:T(1,128)} %bitcast.6, f32[1,256]{1,0:T(1,128)} %bitcast.7, s32[1,256]{1,0:T(1,128)} %bitcast.8, s32[1,256]{1,0:T(1,128)} %bitcast.9, f32[64,128]{1,0:T(8,128)} %decay_hbm.1, f32[128,128]{1,0:T(8,128)} %mix_hbm.1, ...), custom_call_target="tpu_custom_call" | custom-call | tf_op jit(solution)/shard_map/pallas_call | solution.py:370
  29.4 1.4 %copy.11 = f32[64,128]{1,0:T(8,128)} copy(f32[64,128]{1,0:T(8,128)} %shard_map.91) | data formatting | bytes 65536

commit v2 on v1

--- a/solution.py
+++ b/solution.py
@@ -80,7 +80,7 @@
     rows_hbm, prec_hbm, sens_hbm, value_hbm, block_hbm, offset_hbm, decay_hbm, mix_hbm, combine_hbm,
     out_ref,
     rows_ref, prec_ref, sens_ref, value_ref, block_ref, offset_ref, decay_ref, mix_ref, combine_ref, loads,
-    part, got1, red1, got2, info, maps1, vecs1, maps2, vecs2, smooth, pairs, rows2,
+    part, got1, red1, got2, info, maps1, vecs1, maps2, vecs2, smooth, pairs, rows2, edge,
     s_i1, r_i1, s_i2, r_i2, s_i3, r_i3, s_m1, r_m1, s_v1, r_v1, s_m2, r_m2, s_v2, r_v2,
 ):
     sources = (mix_hbm, sens_hbm, value_hbm, prec_hbm, block_hbm, offset_hbm, rows_hbm, decay_hbm, combine_hbm)
@@ -108,11 +108,20 @@
     def at_outer(k):
         return {"tm": k * inner + mine, "sensor": core}
 
+    def at_cross(k):
+        return {"tm": (outer - 1 - group) * inner + k, "sensor": core}
+
     barrier = pltpu.get_barrier_semaphore()
     for r in range(1, spots):
         pl.semaphore_signal(barrier, inc=1, device_id=at_spot(lax.rem(spot + r, spots)), device_id_type=MESH)
     for r in range(1, outer):
         pl.semaphore_signal(barrier, inc=1, device_id=at_outer(lax.rem(group + r, outer)), device_id_type=MESH)
+
+    greeted = spots - 1 + outer - 1
+    if outer == 2:
+        for r in range(1, inner):
+            pl.semaphore_signal(barrier, inc=1, device_id=at_cross(lax.rem(mine + r, inner)), device_id_type=MESH)
+        greeted += inner - 1
 
     for copy in copies_in:
         copy.wait()
@@ -133,7 +142,7 @@
             hot.append(jnp.where(hit, 1.0, 0.0).astype(BF16))
             prec = prec + jnp.where(hit, prec_ref[:, t * width : (t + 1) * width], 0.0)
         picked = picked + dot(cat(hot, 1), lhs2(rows_ref[k * width : (k + 2) * width, :]))
-        if k % 4 == 0 and ROTATION_ITERS - left < early - 2:
+        if k % 4 == 0 and ROTATION_ITERS - left < early - 4:
             matrix, left = polish_step(matrix), left - 1
     gain = values * jnp.sum(prec, axis=1, keepdims=True)
     contrib = (halves(picked) * gain).astype(BF16)
@@ -145,10 +154,10 @@
     line = lax.broadcasted_iota(jnp.int32, (size, obs), 0)
     for s in range(spots):
         part[s] = dot(jnp.where(line == place - s * size, 1.0, 0.0).astype(BF16), contrib).astype(BF16)
-        if s % (spots // 2) == 0 and ROTATION_ITERS - left < early:
+        if s % (spots // 4) == 0 and ROTATION_ITERS - left < early:
             matrix, left = polish_step(matrix), left - 1
 
-    pl.semaphore_wait(barrier, spots - 1 + outer - 1)
+    pl.semaphore_wait(barrier, greeted)
 
     sent1 = []
     for r in range(1, spots):
@@ -266,72 +275,118 @@
     def eight(f, b):
         return cat([f, b, jnp.zeros((6, width), F32)], 0)
 
-    vecs1[mine] = eight(fronts[-1][0], tails[-1][0])
+    depths = inner.bit_length() - 1
+
+    def group_maps():
+        tree = [[maps1[k].astype(F32) for k in range(inner)]]
+        bases, base = [], 0
+        while len(tree[-1]) > (1 if outer > 2 else 2):
+            last = tree[-1]
+            tree.append([mm(last[k], last[k + 1]) for k in range(0, len(last), 2)])
+            bases.append(base)
+            for k, m in enumerate(tree[-1]):
+                pairs[base + k] = m
+            base += len(tree[-1])
+        return tree, bases
+
+    def group_vectors(tree, top):
+        f = [vecs1[k][0:1] for k in range(inner)]
+        b = [vecs1[k][1:2] for k in range(inner)]
+        base, bases = 0, []
+        for depth in range(top):
+            m = tree[depth]
+            f, b = (
+                [mm(f[k], m[k + 1]) + f[k + 1] for k in range(0, len(m), 2)],
+                [mm_nt(b[k + 1], m[k]) + b[k] for k in range(0, len(m), 2)],
+            )
+            bases.append(base)
+            for k in range(len(f)):
+                rows2[base + k] = eight(f[k], b[k])
+            base += len(f)
+        return f, b, bases
+
+    def walk(bases):
+        for depth in reversed(range(depths)):
+            node = lax.div(mine, 1 << depth)
+            bit = lax.rem(node, 2)
+            even = node - bit
+            if depth == 0:
+                yield depth, bit, even, maps1[even].astype(F32), maps1[even + 1].astype(F32)
+            else:
+                at = bases[depth - 1] + even
+                yield depth, bit, even, pairs[at], pairs[at + 1]
+
+    def walk_maps(bases):
+        eye = (
+            lax.broadcasted_iota(jnp.int32, (width, width), 0) == lax.broadcasted_iota(jnp.int32, (width, width), 1)
+        ).astype(F32)
+        to_here, from_here = eye, eye
+        for _, bit, _, m0, m1 in walk(bases):
+            to_here = jnp.where(bit == 1, mm(to_here, m0), to_here)
+            from_here = jnp.where(bit == 0, mm_nt(from_here, m1), from_here)
+        return to_here, from_here
+
+    def walk_vectors(bases, rows_bases):
+        near_f, near_b = jnp.zeros((1, width), F32), jnp.zeros((1, width), F32)
+        for depth, bit, even, m0, m1 in walk(bases):
+            if depth == 0:
+                v0, v1 = vecs1[even], vecs1[even + 1]
+            else:
+                at = rows_bases[depth - 1] + even
+                v0, v1 = rows2[at], rows2[at + 1]
+            near_f = jnp.where(bit == 1, mm(near_f, m0) + v0[0:1], near_f)
+            near_b = jnp.where(bit == 0, mm_nt(near_b, m1) + v1[1:2], near_b)
+        return near_f, near_b
+
+    zero = jnp.zeros((1, width), F32)
+    own_f, own_b = fronts[-1][0], tails[-1][0]
+    vecs1[mine] = eight(own_f, own_b)
     sent_v1 = exchange(vecs1.at[mine], vecs1, mine, inner, s_v1, r_v1, at_inner)
     for copy in sent_m1:
         copy.wait()
-
-    tree = [[maps1[k].astype(F32) for k in range(inner)]]
-    bases, base = [], 0
-    while len(tree[-1]) > (1 if outer > 2 else 2):
-        last = tree[-1]
-        tree.append([mm(last[k], last[k + 1]) for k in range(0, len(last), 2)])
-        bases.append(base)
-        for k, m in enumerate(tree[-1]):
-            pairs[base + k] = m
-        base += len(tree[-1])
-    sent_m2 = []
-    if outer > 2:
+    tree, bases = group_maps()
+    if outer == 2:
+        to_here, from_here = walk_maps(bases)
+        edge[...] = eight(mm_nt(own_f, from_here), mm_nt(own_b, to_here))
+        sent_v2 = []
+        for r in range(inner):
+            copy = pltpu.make_async_remote_copy(
+                edge, vecs2.at[mine], s_v2.at[r], r_v2.at[r],
+                device_id=at_cross(lax.rem(mine + r, inner)), device_id_type=MESH,
+            )
+            copy.start()
+            sent_v2.append(copy)
+        for copy in sent_v1:
+            copy.wait()
+        _, _, rows_bases = group_vectors(tree, depths - 1)
+        near_f, near_b = walk_vectors(bases, rows_bases)
+        for copy in sent_v2:
+            copy.wait()
+        outside = vecs2[0]
+        for k in range(1, inner):
+            outside = outside + vecs2[k]
+        enter = jnp.where(group > 0, outside[0:1], zero)
+        arrive = jnp.where(group < 1, outside[1:2], zero)
+    else:
         maps2[group] = tree[-1][0]
         sent_m2 = exchange(maps2.at[group], maps2, group, outer, s_m2, r_m2, at_outer)
-    for copy in sent_v1:
-        copy.wait()
-    f = [vecs1[k][0:1] for k in range(inner)]
-    b = [vecs1[k][1:2] for k in range(inner)]
-    depths, base = inner.bit_length() - 1, 0
-    rows2_bases = []
-    for depth in range(depths):
-        m = tree[depth]
-        f, b = (
-            [mm(f[k], m[k + 1]) + f[k + 1] for k in range(0, len(m), 2)],
-            [mm_nt(b[k + 1], m[k]) + b[k] for k in range(0, len(m), 2)],
-        )
-        rows2_bases.append(base)
-        for k in range(len(f)):
-            rows2[base + k] = eight(f[k], b[k])
-        base += len(f)
-    vecs2[group] = eight(f[0], b[0])
-    sent_v2 = exchange(vecs2.at[group], vecs2, group, outer, s_v2, r_v2, at_outer)
-
-    eye = (
-        lax.broadcasted_iota(jnp.int32, (width + 8, width), 0) == lax.broadcasted_iota(jnp.int32, (width + 8, width), 1)
-    ).astype(F32)
-    to_here, from_here = eye, eye
-    for depth in reversed(range(depths)):
-        node = lax.div(mine, 1 << depth)
-        bit = lax.rem(node, 2)
-        even = node - bit
-        if depth == 0:
-            m0, m1, v0, v1 = maps1[even].astype(F32), maps1[even + 1].astype(F32), vecs1[even], vecs1[even + 1]
-        else:
-            m0, m1 = pairs[bases[depth - 1] + even], pairs[bases[depth - 1] + even + 1]
-            v0, v1 = rows2[rows2_bases[depth - 1] + even], rows2[rows2_bases[depth - 1] + even + 1]
-        pad = jnp.zeros((width, width), F32)
-        to_here = jnp.where(bit == 1, mm(to_here, m0) + cat([pad, v0], 0), to_here)
-        from_here = jnp.where(bit == 0, mm_nt(from_here, m1) + cat([pad, v1], 0), from_here)
-
-    for copy in sent_m2 + sent_v2:
-        copy.wait()
-
-    zero = jnp.zeros((1, width), F32)
-    enter = jnp.where(group > 0, vecs2[0][0:1], zero)
-    arrive = jnp.where(group < outer - 1, vecs2[outer - 1][1:2], zero)
-    for k in range(1, outer - 1):
-        enter = jnp.where(k < group, mm(enter, maps2[k]) + vecs2[k][0:1], enter)
-        j = outer - 1 - k
-        arrive = jnp.where(j > group, mm_nt(arrive, maps2[j]) + vecs2[j][1:2], arrive)
-    enter = mm(enter, to_here[:width]) + to_here[width : width + 1]
-    arrive = mm(arrive, from_here[:width]) + from_here[width + 1 : width + 2]
+        for copy in sent_v1:
+            copy.wait()
+        f, b, rows_bases = group_vectors(tree, depths)
+        vecs2[group] = eight(f[0], b[0])
+        sent_v2 = exchange(vecs2.at[group], vecs2, group, outer, s_v2, r_v2, at_outer)
+        to_here, from_here = walk_maps(bases)
+        near_f, near_b = walk_vectors(bases, rows_bases)
+        for copy in sent_m2 + sent_v2:
+            copy.wait()
+        enter = jnp.where(group > 0, vecs2[0][0:1], zero)
+        arrive = jnp.where(group < outer - 1, vecs2[outer - 1][1:2], zero)
+        for k in range(1, outer - 1):
+            enter = jnp.where(k < group, mm(enter, maps2[k]) + vecs2[k][0:1], enter)
+            j = outer - 1 - k
+            arrive = jnp.where(j > group, mm_nt(arrive, maps2[j]) + vecs2[j][1:2], arrive)
+    enter = mm(enter, to_here) + near_f
+    arrive = mm(arrive, from_here) + near_b
 
     starts, ends = [enter], [arrive]
     for depth in reversed(range(len(levels) - 1)):
@@ -360,7 +415,7 @@
     outer = peers // inner
     steps, width = decay.shape
     half = steps // cores
-    spots = inner * cores
+    spots, slots = inner * cores, max(inner, outer)
     dma = pltpu.SemaphoreType.DMA
     obs = obs_sensor.shape[0]
     arrays = (
@@ -368,7 +423,7 @@
         obs_block.reshape(1, obs), obs_offset.reshape(1, obs), decay, mix_raw, combine,
     )
     return pl.pallas_call(
-        functools.partial(kernel, inner, outer, cores, 6),
+        functools.partial(kernel, inner, outer, cores, 8),
         out_shape=jax.ShapeDtypeStruct((steps, width), F32),
         in_specs=[pl.BlockSpec(memory_space=pltpu.HBM)] * 9,
         out_specs=pl.BlockSpec(memory_space=pltpu.VMEM),
@@ -382,13 +437,14 @@
             pltpu.VMEM((inner, width, width), BF16),
             pltpu.VMEM((inner, 8, width), F32),
             pltpu.VMEM((outer, width, width), F32),
-            pltpu.VMEM((outer, 8, width), F32),
+            pltpu.VMEM((slots, 8, width), F32),
             pltpu.VMEM((steps, width), F32),
             pltpu.VMEM((inner, width, width), F32),
             pltpu.VMEM((inner, 8, width), F32),
+            pltpu.VMEM((8, width), F32),
             dma((spots,)), dma((spots,)), dma((outer,)), dma((outer,)), dma, dma,
             dma((inner,)), dma((inner,)), dma((inner,)), dma((inner,)),
-            dma((outer,)), dma((outer,)), dma((outer,)), dma((outer,)),
+            dma((outer,)), dma((outer,)), dma((slots,)), dma((slots,)),
         ],
         compiler_params=pltpu.CompilerParams(
             collective_id=0, has_side_effects=True, vmem_limit_bytes=60 * 1024 * 1024

time: 31 us -> 31.9 us (1.029)
  Pallas kernels: 29.4 us -> 30.3 us
    pallas_call x1, Pallas kernels: 29.4 us -> 30.3 us  [local(): pl.pallas_call(functools.partial(kernel, inner, outer, cores, 8), out_sha...]
where the time goes in v2:
time: 31.9 us; the launch traced here: 31.7 us
  Pallas kernels  30.3 us (95%)
  local copies, waits for them, and re-layouts  1.38 us (4%)
    pallas_call x1, Pallas kernels, local(): pl.pallas_call(functools.partial(kernel, inner, outer, cores, 8), out_sha...  30.3 us
    unnamed x1, local copies, waits for them, and re-layouts  1.38 us

profile of v2, /device:TPU:0, one launch (start us, length us, event | category | flops | bytes accessed | tf_op | source)
XLA Modules:
  0.0 31.7 jit_solution(806922946994313643)
XLA Ops:
  0.0 30.3 %shard_map.91 = f32[64,128]{1,0:T(8,128)} custom-call(f32[2048,128]{1,0:T(8,128)} %rows_hbm.1, f32[1,2048]{1,0:T(1,128)} %bitcast.5, s32[1,256]{1,0:T(1,128)} %bitcast.6, f32[1,256]{1,0:T(1,128)} %bitcast.7, s32[1,256]{1,0:T(1,128)} %bitcast.8, s32[1,256]{1,0:T(1,128)} %bitcast.9, f32[64,128]{1,0:T(8,128)} %decay_hbm.1, f32[128,128]{1,0:T(8,128)} %mix_hbm.1, ...), custom_call_target="tpu_custom_call" | custom-call | tf_op jit(solution)/shard_map/pallas_call | solution.py:425
  30.3 1.4 %copy.11 = f32[64,128]{1,0:T(8,128)} copy(f32[64,128]{1,0:T(8,128)} %shard_map.91) | data formatting | bytes 65536

commit v3 on v2

--- a/solution.py
+++ b/solution.py
@@ -142,7 +142,7 @@
             hot.append(jnp.where(hit, 1.0, 0.0).astype(BF16))
             prec = prec + jnp.where(hit, prec_ref[:, t * width : (t + 1) * width], 0.0)
         picked = picked + dot(cat(hot, 1), lhs2(rows_ref[k * width : (k + 2) * width, :]))
-        if k % 4 == 0 and ROTATION_ITERS - left < early - 4:
+        if ROTATION_ITERS - left < early - 4:
             matrix, left = polish_step(matrix), left - 1
     gain = values * jnp.sum(prec, axis=1, keepdims=True)
     contrib = (halves(picked) * gain).astype(BF16)
@@ -182,8 +182,26 @@
         return [halves(dot(lhs2(m), ahead)) * decay_row(c * CHUNK + j) for c, m in enumerate(maps)]
 
     maps = [turned * decay_row(c * CHUNK) for c in range(chunks)]
-    for j in range(1, 3):
+    for j in range(1, CHUNK):
         maps = advance(maps, j)
+    levels = [maps]
+    while len(levels[-1]) > 1:
+        last = levels[-1]
+        levels.append([mm(last[k], last[k + 1]) for k in range(0, len(last), 2)])
+
+    def exchange(source, slots, me, count, send, recv, place_of):
+        copies = []
+        for r in range(1, count):
+            copy = pltpu.make_async_remote_copy(
+                source, slots.at[me], send.at[r], recv.at[r],
+                device_id=place_of(lax.rem(me + r, count)), device_id_type=MESH,
+            )
+            copy.start()
+            copies.append(copy)
+        return copies
+
+    maps1[mine] = levels[-1][0].astype(maps1.dtype)
+    sent_m1 = exchange(maps1.at[mine], maps1, mine, inner, s_m1, r_m1, at_inner)
 
     for copy in sent1:
         copy.wait()
@@ -201,8 +219,6 @@
         sent2.append(copy)
     got2[group] = red1[group]
 
-    for j in range(3, CHUNK):
-        maps = advance(maps, j)
     for copy in sent2:
         copy.wait()
     total = got2[0]
@@ -214,63 +230,6 @@
         info.at[core], info.at[core], s_i3, r_i3, device_id={"tm": tm, "sensor": other}, device_id_type=MESH
     )
     copy3.start()
-
-    levels = [maps]
-    while len(levels[-1]) > 1:
-        last = levels[-1]
-        levels.append([mm(last[k], last[k + 1]) for k in range(0, len(last), 2)])
-
-    def exchange(source, slots, me, count, send, recv, place_of):
-        copies = []
-        for r in range(1, count):
-            copy = pltpu.make_async_remote_copy(
-                source, slots.at[me], send.at[r], recv.at[r],
-                device_id=place_of(lax.rem(me + r, count)), device_id_type=MESH,
-            )
-            copy.start()
-            copies.append(copy)
-        return copies
-
-    maps1[mine] = levels[-1][0].astype(maps1.dtype)
-    sent_m1 = exchange(maps1.at[mine], maps1, mine, inner, s_m1, r_m1, at_inner)
-
-    copy3.wait()
-
-    def strided(ref, j):
-        return ref[pl.ds(j, chunks, stride=CHUNK), :]
-
-    for c in range(cores):
-        smooth[c * half : (c + 1) * half, :] = info[c]
-    news = [strided(smooth, j) for j in range(CHUNK)]
-    fades = [strided(decay_ref, j) for j in range(CHUNK)]
-
-    def forward_scan(enter):
-        out, state = [], enter
-        for j in range(CHUNK):
-            if state is None:
-                state = news[j]
-            else:
-                state = halves(dot(lhs2(state), ahead)) * fades[j] + news[j]
-            out.append(state)
-        return out
-
-    def backward_scan(arrive):
-        out, message = [None] * CHUNK, arrive
-        for j in reversed(range(CHUNK)):
-            value = news[j] if message is None else news[j] + message
-            out[j] = value
-            if j > 0 or arrive is None:
-                message = halves(dot(lhs2(value * fades[j]), back))
-        return out, message
-
-    first = forward_scan(None)[-1]
-    second = backward_scan(None)[1]
-    fronts = [[first[c : c + 1] for c in range(chunks)]]
-    tails = [[second[c : c + 1] for c in range(chunks)]]
-    for depth in range(len(levels) - 1):
-        f, b, m = fronts[-1], tails[-1], levels[depth]
-        fronts.append([mm(f[k], m[k + 1]) + f[k + 1] for k in range(0, len(m), 2)])
-        tails.append([mm_nt(b[k + 1], m[k]) + b[k] for k in range(0, len(m), 2)])
 
     def eight(f, b):
         return cat([f, b, jnp.zeros((6, width), F32)], 0)
@@ -338,15 +297,53 @@
             near_b = jnp.where(bit == 0, mm_nt(near_b, m1) + v1[1:2], near_b)
         return near_f, near_b
 
+    for copy in sent_m1:
+        copy.wait()
+    tree, bases = group_maps()
+    to_here, from_here = walk_maps(bases)
+    copy3.wait()
+
+    def strided(ref, j):
+        return ref[pl.ds(j, chunks, stride=CHUNK), :]
+
+    for c in range(cores):
+        smooth[c * half : (c + 1) * half, :] = info[c]
+    news = [strided(smooth, j) for j in range(CHUNK)]
+    fades = [strided(decay_ref, j) for j in range(CHUNK)]
+
+    def forward_scan(enter):
+        out, state = [], enter
+        for j in range(CHUNK):
+            if state is None:
+                state = news[j]
+            else:
+                state = halves(dot(lhs2(state), ahead)) * fades[j] + news[j]
+            out.append(state)
+        return out
+
+    def backward_scan(arrive):
+        out, message = [None] * CHUNK, arrive
+        for j in reversed(range(CHUNK)):
+            value = news[j] if message is None else news[j] + message
+            out[j] = value
+            if j > 0 or arrive is None:
+                message = halves(dot(lhs2(value * fades[j]), back))
+        return out, message
+
+    first = forward_scan(None)[-1]
+    second = backward_scan(None)[1]
+    fronts = [[first[c : c + 1] for c in range(chunks)]]
+    tails = [[second[c : c + 1] for c in range(chunks)]]
+    for depth in range(len(levels) - 1):
+        f, b, m = fronts[-1], tails[-1], levels[depth]
+        fronts.append([mm(f[k], m[k + 1]) + f[k + 1] for k in range(0, len(m), 2)])
+        tails.append([mm_nt(b[k + 1], m[k]) + b[k] for k in range(0, len(m), 2)])
+
     zero = jnp.zeros((1, width), F32)
     own_f, own_b = fronts[-1][0], tails[-1][0]
     vecs1[mine] = eight(own_f, own_b)
     sent_v1 = exchange(vecs1.at[mine], vecs1, mine, inner, s_v1, r_v1, at_inner)
-    for copy in sent_m1:
-        copy.wait()
-    tree, bases = group_maps()
     if outer == 2:
-        to_here, from_here = walk_maps(bases)
         edge[...] = eight(mm_nt(own_f, from_here), mm_nt(own_b, to_here))
         sent_v2 = []
         for r in range(inner):
@@ -375,7 +372,6 @@
         f, b, rows_bases = group_vectors(tree, depths)
         vecs2[group] = eight(f[0], b[0])
         sent_v2 = exchange(vecs2.at[group], vecs2, group, outer, s_v2, r_v2, at_outer)
-        to_here, from_here = walk_maps(bases)
         near_f, near_b = walk_vectors(bases, rows_bases)
         for copy in sent_m2 + sent_v2:
             copy.wait()
@@ -423,7 +419,7 @@
         obs_block.reshape(1, obs), obs_offset.reshape(1, obs), decay, mix_raw, combine,
     )
     return pl.pallas_call(
-        functools.partial(kernel, inner, outer, cores, 8),
+        functools.partial(kernel, inner, outer, cores, 12),
         out_shape=jax.ShapeDtypeStruct((steps, width), F32),
         in_specs=[pl.BlockSpec(memory_space=pltpu.HBM)] * 9,
         out_specs=pl.BlockSpec(memory_space=pltpu.VMEM),

time: 31.9 us -> 30.7 us (0.962)
  Pallas kernels: 30.3 us -> 29.1 us
    pallas_call x1, Pallas kernels: 30.3 us -> 29.1 us  [local(): pl.pallas_call(functools.partial(kernel, inner, outer, cores, 12), out_sh...]
where the time goes in v3:
time: 30.7 us; the launch traced here: 30.5 us
  Pallas kernels  29.1 us (95%)
  local copies, waits for them, and re-layouts  1.38 us (4%)
    pallas_call x1, Pallas kernels, local(): pl.pallas_call(functools.partial(kernel, inner, outer, cores, 12), out_sh...  29.1 us
    unnamed x1, local copies, waits for them, and re-layouts  1.38 us

profile of v3, /device:TPU:0, one launch (start us, length us, event | category | flops | bytes accessed | tf_op | source)
XLA Modules:
  0.0 30.5 jit_solution(3108255982087149504)
XLA Ops:
  0.0 29.1 %shard_map.91 = f32[64,128]{1,0:T(8,128)} custom-call(f32[2048,128]{1,0:T(8,128)} %rows_hbm.1, f32[1,2048]{1,0:T(1,128)} %bitcast.5, s32[1,256]{1,0:T(1,128)} %bitcast.6, f32[1,256]{1,0:T(1,128)} %bitcast.7, s32[1,256]{1,0:T(1,128)} %bitcast.8, s32[1,256]{1,0:T(1,128)} %bitcast.9, f32[64,128]{1,0:T(8,128)} %decay_hbm.1, f32[128,128]{1,0:T(8,128)} %mix_hbm.1, ...), custom_call_target="tpu_custom_call" | custom-call | tf_op jit(solution)/shard_map/pallas_call | solution.py:421
  29.1 1.4 %copy.11 = f32[64,128]{1,0:T(8,128)} copy(f32[64,128]{1,0:T(8,128)} %shard_map.91) | data formatting | bytes 65536

commit v4 on v3

--- a/solution.py
+++ b/solution.py
@@ -80,7 +80,7 @@
     rows_hbm, prec_hbm, sens_hbm, value_hbm, block_hbm, offset_hbm, decay_hbm, mix_hbm, combine_hbm,
     out_ref,
     rows_ref, prec_ref, sens_ref, value_ref, block_ref, offset_ref, decay_ref, mix_ref, combine_ref, loads,
-    part, got1, red1, got2, info, maps1, vecs1, maps2, vecs2, smooth, pairs, rows2, edge,
+    part, got1, red1, got2, info, maps1, vecs1, maps2, vecs2, smooth, pairs, rows2,
     s_i1, r_i1, s_i2, r_i2, s_i3, r_i3, s_m1, r_m1, s_v1, r_v1, s_m2, r_m2, s_v2, r_v2,
 ):
     sources = (mix_hbm, sens_hbm, value_hbm, prec_hbm, block_hbm, offset_hbm, rows_hbm, decay_hbm, combine_hbm)
@@ -108,9 +108,6 @@
     def at_outer(k):
         return {"tm": k * inner + mine, "sensor": core}
 
-    def at_cross(k):
-        return {"tm": (outer - 1 - group) * inner + k, "sensor": core}
-
     barrier = pltpu.get_barrier_semaphore()
     for r in range(1, spots):
         pl.semaphore_signal(barrier, inc=1, device_id=at_spot(lax.rem(spot + r, spots)), device_id_type=MESH)
@@ -118,11 +115,6 @@
         pl.semaphore_signal(barrier, inc=1, device_id=at_outer(lax.rem(group + r, outer)), device_id_type=MESH)
 
     greeted = spots - 1 + outer - 1
-    if outer == 2:
-        for r in range(1, inner):
-            pl.semaphore_signal(barrier, inc=1, device_id=at_cross(lax.rem(mine + r, inner)), device_id_type=MESH)
-        greeted += inner - 1
-
     for copy in copies_in:
         copy.wait()
 
@@ -343,44 +335,24 @@
     own_f, own_b = fronts[-1][0], tails[-1][0]
     vecs1[mine] = eight(own_f, own_b)
     sent_v1 = exchange(vecs1.at[mine], vecs1, mine, inner, s_v1, r_v1, at_inner)
-    if outer == 2:
-        edge[...] = eight(mm_nt(own_f, from_here), mm_nt(own_b, to_here))
-        sent_v2 = []
-        for r in range(inner):
-            copy = pltpu.make_async_remote_copy(
-                edge, vecs2.at[mine], s_v2.at[r], r_v2.at[r],
-                device_id=at_cross(lax.rem(mine + r, inner)), device_id_type=MESH,
-            )
-            copy.start()
-            sent_v2.append(copy)
-        for copy in sent_v1:
-            copy.wait()
-        _, _, rows_bases = group_vectors(tree, depths - 1)
-        near_f, near_b = walk_vectors(bases, rows_bases)
-        for copy in sent_v2:
-            copy.wait()
-        outside = vecs2[0]
-        for k in range(1, inner):
-            outside = outside + vecs2[k]
-        enter = jnp.where(group > 0, outside[0:1], zero)
-        arrive = jnp.where(group < 1, outside[1:2], zero)
-    else:
+    sent_m2 = []
+    if outer > 2:
         maps2[group] = tree[-1][0]
         sent_m2 = exchange(maps2.at[group], maps2, group, outer, s_m2, r_m2, at_outer)
-        for copy in sent_v1:
-            copy.wait()
-        f, b, rows_bases = group_vectors(tree, depths)
-        vecs2[group] = eight(f[0], b[0])
-        sent_v2 = exchange(vecs2.at[group], vecs2, group, outer, s_v2, r_v2, at_outer)
-        near_f, near_b = walk_vectors(bases, rows_bases)
-        for copy in sent_m2 + sent_v2:
-            copy.wait()
-        enter = jnp.where(group > 0, vecs2[0][0:1], zero)
-        arrive = jnp.where(group < outer - 1, vecs2[outer - 1][1:2], zero)
-        for k in range(1, outer - 1):
-            enter = jnp.where(k < group, mm(enter, maps2[k]) + vecs2[k][0:1], enter)
-            j = outer - 1 - k
-            arrive = jnp.where(j > group, mm_nt(arrive, maps2[j]) + vecs2[j][1:2], arrive)
+    for copy in sent_v1:
+        copy.wait()
+    f, b, rows_bases = group_vectors(tree, depths)
+    vecs2[group] = eight(f[0], b[0])
+    sent_v2 = exchange(vecs2.at[group], vecs2, group, outer, s_v2, r_v2, at_outer)
+    near_f, near_b = walk_vectors(bases, rows_bases)
+    for copy in sent_m2 + sent_v2:
+        copy.wait()
+    enter = jnp.where(group > 0, vecs2[0][0:1], zero)
+    arrive = jnp.where(group < outer - 1, vecs2[outer - 1][1:2], zero)
+    for k in range(1, outer - 1):
+        enter = jnp.where(k < group, mm(enter, maps2[k]) + vecs2[k][0:1], enter)
+        j = outer - 1 - k
+        arrive = jnp.where(j > group, mm_nt(arrive, maps2[j]) + vecs2[j][1:2], arrive)
     enter = mm(enter, to_here) + near_f
     arrive = mm(arrive, from_here) + near_b
 
@@ -437,7 +409,6 @@
             pltpu.VMEM((steps, width), F32),
             pltpu.VMEM((inner, width, width), F32),
             pltpu.VMEM((inner, 8, width), F32),
-            pltpu.VMEM((8, width), F32),
             dma((spots,)), dma((spots,)), dma((outer,)), dma((outer,)), dma, dma,
             dma((inner,)), dma((inner,)), dma((inner,)), dma((inner,)),
             dma((outer,)), dma((outer,)), dma((slots,)), dma((slots,)),

time: 30.7 us -> 32.6 us (1.062)
  Pallas kernels: 29.1 us -> 31 us
    pallas_call x1, Pallas kernels: 29.1 us -> 31 us  [local(): pl.pallas_call(functools.partial(kernel, inner, outer, cores, 12), out_sh...]
where the time goes in v4:
time: 32.6 us; the launch traced here: 32.4 us
  Pallas kernels  31 us (95%)
  local copies, waits for them, and re-layouts  1.38 us (4%)
    pallas_call x1, Pallas kernels, local(): pl.pallas_call(functools.partial(kernel, inner, outer, cores, 12), out_sh...  31 us
    unnamed x1, local copies, waits for them, and re-layouts  1.38 us

profile of v4, /device:TPU:0, one launch (start us, length us, event | category | flops | bytes accessed | tf_op | source)
XLA Modules:
  0.0 32.4 jit_solution(14623082898711888513)
XLA Ops:
  0.0 31.0 %shard_map.91 = f32[64,128]{1,0:T(8,128)} custom-call(f32[2048,128]{1,0:T(8,128)} %rows_hbm.1, f32[1,2048]{1,0:T(1,128)} %bitcast.5, s32[1,256]{1,0:T(1,128)} %bitcast.6, f32[1,256]{1,0:T(1,128)} %bitcast.7, s32[1,256]{1,0:T(1,128)} %bitcast.8, s32[1,256]{1,0:T(1,128)} %bitcast.9, f32[64,128]{1,0:T(8,128)} %decay_hbm.1, f32[128,128]{1,0:T(8,128)} %mix_hbm.1, ...), custom_call_target="tpu_custom_call" | custom-call | tf_op jit(solution)/shard_map/pallas_call | solution.py:393
  31.0 1.4 %copy.11 = f32[64,128]{1,0:T(8,128)} copy(f32[64,128]{1,0:T(8,128)} %shard_map.91) | data formatting | bytes 65536
